TPU v7x, 32 devices: a whole 2x2x4 slice. The times are simulated.
32 devices in a mesh: area: 8 (over y, x, core), layer: 4 (over z).
Axes of the slice: x: 2, y: 2, z: 4, core: 2. Of those that a mesh axis runs over, the one named last changes fastest.
Arguments:
- permeability: float32 [16, 4096, 512], P('layer', 'area'), may hold values from 0.1 to 10
- mobility: float32 [16, 4096, 512], P('layer', 'area'), may hold values from 0.3 to 3
- thickness: float32 [16], P('layer'), may hold values from 0.5 to 2
- caprock: int32 [4096, 512], P('area'), may hold values from 0 to 7
- plume: int32 [4096, 512], P('area'), may hold values from 0 to 15
- storage: float32 [4096, 512], P('area'), may hold values from 1.6 to 16
- source: float32 [4096, 512], P('area'), may hold values from -192 to 192
- pressure_old: float32 [4096, 512], P('area'), may hold values from -6 to 6
Outputs:
- cell_pressure: float32 [16, 4096, 512], P('layer', 'area')
- flux_rows: float32 [16, 4096, 512], P('layer', 'area')
- flux_cols: float32 [16, 4096, 512], P('layer', 'area')
Inputs may be any that keep to these rules, and one draw needn't show every extreme that they name: Layers above layer caprock of a column are sealed rock. CO2 fills the open layers above layer plume of a column; where plume <= caprock a column holds no CO2.
All inputs are finite; a program needn't handle non-finite values.
Results may differ from a plain program's by a relative error of at most 0.0003.
Values sent between devices are 32-bit elements; how exact they have to be, the bound alone decides.
No kernel may reach another device: no remote copies, remote signals or barrier semaphores. Data moves between devices by JAX's collectives and lax.ppermute only.
A program may use at most 128 MiB of HBM per device.

v0:
```python
import jax
import jax.numpy as jnp
from jax import lax
from jax.sharding import PartitionSpec as P

SWEEPS = 3
buoyancy_scale = 0.3
gravity_scale = 0.05
gas_density = 0.7
brine_density = 1.0


def padded_2(block, sides, width):
    for axis, dim in sides:
        count = lax.axis_size(axis)
        forward = [(i, i + 1) for i in range(count - 1)]
        backward = [(target, source) for source, target in forward]
        low = lax.ppermute(
            lax.slice_in_dim(block, block.shape[dim] - width, None, axis=dim), axis, forward
        )
        high = lax.ppermute(lax.slice_in_dim(block, 0, width, axis=dim), axis, backward)
        block = jnp.concatenate([low, block, high], axis=dim)
    return block


def from_behind(block, axis, distance):
    devices = range(lax.axis_size(axis))
    route = [(i - distance, i) for i in devices if i - distance in devices]
    return lax.ppermute(block, axis, route)


def harmonic(near_value, far_value):
    summed = near_value + far_value
    divisor = jnp.where(summed > 0, summed, 1.0)
    return 2.0 * near_value * far_value / divisor


def neighbours(padded, row_count):
    widened = jnp.pad(padded, ((0, 0), (1, 1)))
    return [
        widened[0:row_count, 1:-1],
        widened[2 : row_count + 2, 1:-1],
        widened[1 : row_count + 1, 0:-2],
        widened[1 : row_count + 1, 2:],
    ]


def prepare(summed_pad, storage, source, pressure_old):
    row_count = storage.shape[0]
    trans_pad = summed_pad[0]
    buoy_pad = summed_pad[1]
    drive_pad = buoyancy_scale * summed_pad[2]
    trans_faces = [
        harmonic(trans_pad[1 : row_count + 1], neighbour)
        for neighbour in neighbours(trans_pad, row_count)
    ]
    buoy_faces = [
        harmonic(buoy_pad[1 : row_count + 1], neighbour)
        for neighbour in neighbours(buoy_pad, row_count)
    ]
    drive_centre = drive_pad[1 : row_count + 1]
    gravity_drive = sum(
        (
            face_coef * (neighbour - drive_centre)
            for face_coef, neighbour in zip(buoy_faces, neighbours(drive_pad, row_count))
        )
    )
    right_hand = storage * pressure_old + source + gravity_drive
    diagonal = storage + trans_faces[0] + trans_faces[1] + trans_faces[2] + trans_faces[3]
    return (trans_faces, right_hand, diagonal)


def relax(trans_faces, right_hand, diagonal, padded):
    row_count = right_hand.shape[0]
    inflow = sum(
        (
            face_coef * neighbour
            for face_coef, neighbour in zip(trans_faces, neighbours(padded, row_count))
        )
    )
    return (right_hand + inflow) / diagonal


def column_depths(every_thick, layer_count, caprock, plume, limit):
    block_count = every_thick.shape[0] // layer_count

    def add_block(block, carry):
        height, above = carry
        first = block * layer_count
        thick_block = lax.dynamic_slice_in_dim(every_thick, first, layer_count, 0)[:, None, None]
        depth = first + lax.broadcasted_iota(jnp.int32, (layer_count, 1, 1), 0)
        gas = (depth >= caprock[None]) & (depth < plume[None])
        height = height + jnp.sum(jnp.where(gas, thick_block, 0.0), axis=0)
        above = above + jnp.sum(jnp.where(gas & (depth < limit), thick_block, 0.0), axis=0)
        return (height, above)

    zeros = jnp.zeros(caprock.shape, jnp.float32)
    return lax.fori_loop(0, block_count, add_block, (zeros, zeros))


def local(permeability, mobility, thickness, caprock, plume, storage, source, pressure_old):
    layer_count = permeability.shape[0]
    layer_index = lax.axis_index("layer")
    layers = layer_index * layer_count + lax.broadcasted_iota(jnp.int32, permeability.shape, 0)
    open_cell = layers >= caprock[None]
    gas_cell = open_cell & (layers < plume[None])
    layer_thick = thickness[:, None, None]
    conduct = jnp.where(open_cell, permeability * mobility * layer_thick, 0.0)
    every_thick = lax.all_gather(thickness, "layer", axis=0, tiled=True)
    limit = layer_index * layer_count
    gas_height, gas_above = column_depths(every_thick, layer_count, caprock, plume, limit)
    column_parts = jnp.stack(
        [jnp.sum(conduct, axis=0), jnp.sum(jnp.where(gas_cell, conduct, 0.0), axis=0)]
    )
    summed = lax.psum(column_parts, "layer")
    summed = jnp.concatenate([summed, gas_height[None]], axis=0)
    padded = padded_2(summed, (("area", 1),), 1)
    trans_faces, right_hand, diagonal = prepare(padded, storage, source, pressure_old)
    pressure = pressure_old
    for sweep_index in range(SWEEPS):
        pressure_pad = padded_2(pressure, (("area", 0),), 1)
        pressure = relax(trans_faces, right_hand, diagonal, pressure_pad)
    layer_mass = layer_thick * jnp.where(gas_cell, gas_density, brine_density)
    depth_all = lax.broadcasted_iota(jnp.int32, every_thick.shape, 0)
    thick_over = jnp.sum(jnp.where(depth_all < limit, every_thick, 0.0))
    mass_over = thick_over - (brine_density - gas_density) * gas_above
    hydro_head = mass_over[None] + jnp.cumsum(layer_mass, axis=0) - 0.5 * layer_mass
    cell_pressure = pressure[None] + gravity_scale * hydro_head
    edge_rows = jnp.stack([conduct[:, 0, :], cell_pressure[:, 0, :]])
    beyond = from_behind(edge_rows, "area", -1)
    next_conduct = jnp.concatenate([conduct[:, 1:, :], beyond[0][:, None, :]], axis=1)
    next_pressure = jnp.concatenate([cell_pressure[:, 1:, :], beyond[1][:, None, :]], axis=1)
    flux_rows = harmonic(conduct, next_conduct) * (cell_pressure - next_pressure)
    side_conduct = jnp.pad(conduct[:, :, 1:], ((0, 0), (0, 0), (0, 1)))
    side_pressure = jnp.pad(cell_pressure[:, :, 1:], ((0, 0), (0, 0), (0, 1)))
    flux_cols = harmonic(conduct, side_conduct) * (cell_pressure - side_pressure)
    return (cell_pressure, flux_rows, flux_cols)


def solution(mesh):
    in_specs = (
        P("layer", "area", None),
        P("layer", "area", None),
        P("layer"),
        P("area", None),
        P("area", None),
        P("area", None),
        P("area", None),
        P("area", None),
    )
    out_specs = (P("layer", "area", None), P("layer", "area", None), P("layer", "area", None))
    return jax.shard_map(local, mesh=mesh, in_specs=in_specs, out_specs=out_specs, check_vma=False)
```

profile of v0, /device:TPU:4, one launch (start us, length us, event | category | flops | bytes accessed | tf_op | source)
XLA Modules:
  0.0 176.6 jit_solution(2895812345910085846)
XLA Ops:
  7.2 0.7 fusion.65
  8.0 1.9 %collective-permute-start.2 = (f32[1,512]{1,0:T(1,128)S(1)}, f32[1,512]{1,0:T(1,128)S(1)}, u32[]{:S(2)}, u32[]{:S(2)}) collective-permute-start(f32[1,512]{1,0:T(1,128)S(1)} %get-tuple-element.191), channel_id=1, source_target_pairs={{0,4},{4,8},{8,12},{12,16},{16,20},{20,24},{24,28},{1,5},{5,9},{9,... | collective-permute-start | bytes 6152 | tf_op jit(solution)/shard_map/ppermute | solution.py:18
  9.9 4.5 %collective-permute-start.3 = (f32[1,512]{1,0:T(1,128)S(1)}, f32[1,512]{1,0:T(1,128)S(1)}, u32[]{:S(2)}, u32[]{:S(2)}) collective-permute-start(f32[1,512]{1,0:T(1,128)S(1)} %get-tuple-element.192), channel_id=1, source_target_pairs={{4,0},{8,4},{12,8},{16,12},{20,16},{24,20},{28,24},{5,1},{9,5},{13... | collective-permute-start | bytes 6152 | tf_op jit(solution)/shard_map/ppermute | solution.py:21
  14.4 7.8 %fusion.59 = (f32[512,512]{1,0:T(8,128)S(1)}, f32[512,512]{1,0:T(8,128)S(1)}, f32[4,512,512]{2,1,0:T(8,128)}) fusion(s32[512,512]{1,0:T(8,128)} %param.14, s32[512,512]{1,0:T(8,128)} %param.13, s32[4]{0:T(128)S(1)} %iota_add_fusion.1, f32[4]{0:T(128)} %param.12, f32[4,512,512]{2,1,0:T(8,128)} %param.10, f32[4,512,512]{2,1,0:T(8,128)} %param.11), kind=kLoop, calls=%fused_computation.138 | loop fusion | flops 8912896 | bytes 16777248 | tf_op jit(solution)/shard_map/reduce_sum | solution.py:113
  22.2 1.5 pad_maximum_fusion.2
  23.8 0.6 dynamic-slice
  25.2 12.4 %all-reduce.8 = f32[16]{0:T(128)S(1)} all-reduce(f32[16]{0:T(128)S(1)} %dynamic-update-slice), channel_id=1, replica_groups=mesh['area'=8,'layer'=4] {'layer'}, use_global_device_ids=true, to_apply=%add.8 | all-reduce | flops 16 | bytes 128
  37.6 12.6 %while.16 = (s32[]{:T(128)}, f32[512,512]{1,0:T(8,128)S(1)}, f32[512,512]{1,0:T(8,128)}, s32[512,512]{1,0:T(8,128)S(1)}, s32[512,512]{1,0:T(8,128)S(1)}, /*index...) while((s32[]{:T(128)}, f32[512,512]{1,0:T(8,128)S(1)}, ...), condition=%wide.region_6.7_spmd.clone, body=%wide.region_3.0_spmd.clone.sunk | while | flops 8912915 | bytes 18874700 | solution.py:98
  37.7 1.3 select_reduce_fusion.4
  39.0 0.7 select_add_fusion.3
  39.8 1.0 copy-done.6
  40.8 1.3 select_reduce_fusion.4
  42.2 0.7 select_add_fusion.3
  42.9 1.0 copy-done.6
  44.0 1.3 select_reduce_fusion.4
  45.3 0.7 select_add_fusion.3
  46.1 1.0 copy-done.6
  47.1 1.3 select_reduce_fusion.4
  48.5 0.7 select_add_fusion.3
  49.2 1.0 copy-done.6
  50.2 0.6 fusion.55
  50.8 59.5 %all-reduce.11.cloned.1.call-done = f32[2,512,512]{2,1,0:T(8,128)} async-done(((f32[2,512,512]{2,1,0:T(8,128)}), f32[2,512,512]{2,1,0:T(8,128)}) %all-reduce.11.cloned.1.call-update) | async-done | bytes 2097168 | tf_op jit(solution)/shard_map/psum | solution.py:115
  110.3 0.9 pad_maximum_fusion.15
  111.3 1.9 %collective-permute-start = (f32[3,1,512]{2,1,0:T(1,128)S(1)}, f32[3,1,512]{2,1,0:T(1,128)S(1)}, u32[]{:S(2)}, u32[]{:S(2)}) collective-permute-start(f32[3,1,512]{2,1,0:T(1,128)S(1)} %get-tuple-element.185), channel_id=1, source_target_pairs={{0,4},{4,8},{8,12},{12,16},{16,20},{20,24},{24,28},{1,5},{5,9},{9,... | collective-permute-start | bytes 18440 | tf_op jit(solution)/shard_map/ppermute | solution.py:18
  113.2 4.5 %collective-permute-start.1 = (f32[3,1,512]{2,1,0:T(1,128)S(1)}, f32[3,1,512]{2,1,0:T(1,128)S(1)}, u32[]{:S(2)}, u32[]{:S(2)}) collective-permute-start(f32[3,1,512]{2,1,0:T(1,128)S(1)} %get-tuple-element.186), channel_id=1, source_target_pairs={{4,0},{8,4},{12,8},{16,12},{20,16},{24,20},{28,24},{5,1},{9,5},{13... | collective-permute-start | bytes 18440 | tf_op jit(solution)/shard_map/ppermute | solution.py:21
  117.8 1.6 select_maximum_fusion.4
  119.5 0.4 pad_maximum_fusion.1
  119.9 0.4 slice_multiply_fusion
  120.3 0.8 copy-done.8
  121.8 6.4 %fusion.46 = (f32[512,512]{1,0:T(8,128)S(1)}, f32[512,512]{1,0:T(8,128)S(1)}, f32[512,512]{1,0:T(8,128)S(1)}, f32[512,512]{1,0:T(8,128)S(1)}) fusion(f32[514,514]{1,0:T(8,128)S(1)} %select_maximum_fusion.4, f32[1,512]{1,0:T(1,128)S(1)} %collective-permute-done.3, f32[512,512]{1,0:T(8,128)S(1)} %copy-done.9, f32[1,512]{1,0:T(1,128)S(1)} %collective-permute-done.2, ...), kind=kLoop, calls=%fused_computation.98 | loop fusion | flops 20709376 | bytes 21037056 | tf_op jit(solution)/shard_map/div | solution.py:81
  128.2 2.2 %collective-permute-start.4 = (f32[1,512]{1,0:T(1,128)S(1)}, f32[1,512]{1,0:T(1,128)S(1)}, u32[]{:S(2)}, u32[]{:S(2)}) collective-permute-start(f32[1,512]{1,0:T(1,128)S(1)} %get-tuple-element.189), channel_id=1, source_target_pairs={{0,4},{4,8},{8,12},{12,16},{16,20},{20,24},{24,28},{1,5},{5,9},{9,... | collective-permute-start | bytes 6152 | tf_op jit(solution)/shard_map/ppermute | solution.py:18
  130.4 4.3 %collective-permute-start.5 = (f32[1,512]{1,0:T(1,128)S(1)}, f32[1,512]{1,0:T(1,128)S(1)}, u32[]{:S(2)}, u32[]{:S(2)}) collective-permute-start(f32[1,512]{1,0:T(1,128)S(1)} %get-tuple-element.190), channel_id=1, source_target_pairs={{4,0},{8,4},{12,8},{16,12},{20,16},{24,20},{28,24},{5,1},{9,5},{13... | collective-permute-start | bytes 6152 | tf_op jit(solution)/shard_map/ppermute | solution.py:21
  134.7 0.7 multiply_subtract_fusion
  135.4 0.5 collective-permute-done.5
  136.0 0.4 select_maximum_fusion.2
  136.4 1.7 fusion.39
  138.2 1.9 %collective-permute-start.6 = (f32[1,512]{1,0:T(1,128)S(1)}, f32[1,512]{1,0:T(1,128)S(1)}, u32[]{:S(2)}, u32[]{:S(2)}) collective-permute-start(f32[1,512]{1,0:T(1,128)S(1)} %get-tuple-element.187), channel_id=1, source_target_pairs={{0,4},{4,8},{8,12},{12,16},{16,20},{20,24},{24,28},{1,5},{5,9},{9,... | collective-permute-start | bytes 6152 | tf_op jit(solution)/shard_map/ppermute | solution.py:18
  140.1 4.7 %collective-permute-start.7 = (f32[1,512]{1,0:T(1,128)S(1)}, f32[1,512]{1,0:T(1,128)S(1)}, u32[]{:S(2)}, u32[]{:S(2)}) collective-permute-start(f32[1,512]{1,0:T(1,128)S(1)} %get-tuple-element.188), channel_id=1, source_target_pairs={{4,0},{8,4},{12,8},{16,12},{20,16},{24,20},{28,24},{5,1},{9,5},{13... | collective-permute-start | bytes 6152 | tf_op jit(solution)/shard_map/ppermute | solution.py:21
  144.8 1.1 collective-permute-done.7
  145.9 0.4 select_maximum_fusion
  146.4 1.7 fusion.32
  148.1 2.2 %multiply_add_fusion = f32[4,512,512]{2,1,0:T(8,128)S(1)} fusion(f32[512,512]{1,0:T(8,128)S(1)} %multiply_subtract_fusion, f32[512,512]{1,0:T(8,128)S(1)} %fusion.32, s32[512,512]{1,0:T(8,128)S(1)} %get-tuple-element.281, f32[4]{0:T(128)S(1)} %copy-done.11, s32[512,512]{1,0:T(8,128)S(1)} %get-tuple-element.280, s32[4]{0:T(128)S(1)} %iota_add_fusion.1), kind=kOutput, calls=%fused_computation.17 | output fusion | flops 18874368 | bytes 8388640 | tf_op jit(solution)/shard_map/jit(cumsum)/reduce_window_sum | solution.py:127
  150.3 4.5 %collective-permute-start.8 = (f32[2,4,512]{2,0,1:T(2,128)S(1)}, f32[2,4,512]{2,0,1:T(2,128)S(1)}, u32[]{:S(2)}, u32[]{:S(2)}) collective-permute-start(f32[2,4,512]{2,0,1:T(2,128)S(1)} %pad_maximum_fusion.13), channel_id=1, source_target_pairs={{4,0},{8,4},{12,8},{16,12},{20,16},{24,20},{28,24},{5,1},{9,5},{13... | collective-permute-start | bytes 49160 | tf_op jit(solution)/shard_map/ppermute | solution.py:29
  154.8 0.7 slice.276
  155.5 1.1 slice.282
  156.6 3.1 %slice.283 = f32[4,512,511]{2,1,0:T(8,128)} slice(f32[4,512,512]{2,1,0:T(8,128)S(1)} %multiply_add_fusion), slice={[0:4], [0:512], [1:512]} | slice | bytes 8372224 | tf_op jit(solution)/shard_map/slice | solution.py:135
  159.7 2.5 %slice.280 = f32[4,511,512]{2,1,0:T(8,128)} slice(f32[4,512,512]{2,1,0:T(8,128)S(1)} %multiply_add_fusion), slice={[0:4], [1:512], [0:512]} | slice | bytes 8372224 | tf_op jit(solution)/shard_map/slice | solution.py:132
  162.3 7.4 %fusion.3 = (f32[4,512,512]{2,1,0:T(8,128)}, f32[4,512,512]{2,1,0:T(8,128)}) fusion(f32[4,512,512]{2,1,0:T(8,128)S(1)} %multiply_add_fusion, f32[4,512,511]{2,1,0:T(8,128)} %slice.283, f32[4,512,512]{2,1,0:T(8,128)S(1)} %copy-done.1, f32[4,512,511]{2,1,0:T(8,128)S(1)} %slice.282, f32[4,1,512]{2,1,0:T(1,128)S(1)} %get-tuple-element.194, ...), kind=kLoop, calls=%fused_computation.14 | loop fusion | flops 17825792 | bytes 33538048 | tf_op jit(solution)/shard_map/mul | solution.py:136
  (65 shorter events, 1.4 us)
Async XLA Ops:
  7.2 103.2 %all-reduce.11.cloned.1.call-start = ((), (), s32[]{:S(2)}) async-start(), calls=%async_computation | async-start | bytes 4194304 | tf_op jit(solution)/shard_map/psum | solution.py:115
  8.0 109.8 %collective-permute-start.2 = (f32[1,512]{1,0:T(1,128)S(1)}, f32[1,512]{1,0:T(1,128)S(1)}, u32[]{:S(2)}, u32[]{:S(2)}) collective-permute-start(f32[1,512]{1,0:T(1,128)S(1)} %get-tuple-element.191), channel_id=1, source_target_pairs={{0,4},{4,8},{8,12},{12,16},{16,20},{20,24},{24,28},{1,5},{5,9},{9,... | collective-permute-start | bytes 6152 | tf_op jit(solution)/shard_map/ppermute | solution.py:18
  9.9 107.9 %collective-permute-start.3 = (f32[1,512]{1,0:T(1,128)S(1)}, f32[1,512]{1,0:T(1,128)S(1)}, u32[]{:S(2)}, u32[]{:S(2)}) collective-permute-start(f32[1,512]{1,0:T(1,128)S(1)} %get-tuple-element.192), channel_id=1, source_target_pairs={{4,0},{8,4},{12,8},{16,12},{20,16},{24,20},{28,24},{5,1},{9,5},{13... | collective-permute-start | bytes 6152 | tf_op jit(solution)/shard_map/ppermute | solution.py:21
  22.2 1.6 copy-start.12
  22.2 2.7 %copy-start.11 = (f32[4]{0:T(128)S(1)}, f32[4]{0:T(128)}, u32[]{:S(2)}) copy-start(f32[4]{0:T(128)} %param.12) | copy-start | bytes 52
  22.2 15.4 %copy-start.2 = (s32[512,512]{1,0:T(8,128)S(1)}, s32[512,512]{1,0:T(8,128)}, u32[]{:S(2)}) copy-start(s32[512,512]{1,0:T(8,128)} %param.13) | copy-start | bytes 3145732
  22.2 15.4 %copy-start.3 = (s32[512,512]{1,0:T(8,128)S(1)}, s32[512,512]{1,0:T(8,128)}, u32[]{:S(2)}) copy-start(s32[512,512]{1,0:T(8,128)} %param.14) | copy-start | bytes 3145732
  37.6 1.4 copy-start.5
  39.8 1.0 copy-start.6
  40.8 1.4 copy-start.5
  42.9 1.0 copy-start.6
  43.9 1.4 copy-start.5
  46.1 1.0 copy-start.6
  47.0 1.4 copy-start.5
  49.2 1.0 copy-start.6
  110.3 9.1 %copy-start.4 = (f32[2,512,512]{2,1,0:T(8,128)S(1)}, f32[2,512,512]{2,1,0:T(8,128)}, u32[]{:S(2)}) copy-start(f32[2,512,512]{2,1,0:T(8,128)} %all-reduce.11.cloned.1.call-done) | copy-start | bytes 6291460
  111.3 8.2 %collective-permute-start = (f32[3,1,512]{2,1,0:T(1,128)S(1)}, f32[3,1,512]{2,1,0:T(1,128)S(1)}, u32[]{:S(2)}, u32[]{:S(2)}) collective-permute-start(f32[3,1,512]{2,1,0:T(1,128)S(1)} %get-tuple-element.185), channel_id=1, source_target_pairs={{0,4},{4,8},{8,12},{12,16},{16,20},{20,24},{24,28},{1,5},{5,9},{9,... | collective-permute-start | bytes 18440 | tf_op jit(solution)/shard_map/ppermute | solution.py:18
  113.2 6.2 %collective-permute-start.1 = (f32[3,1,512]{2,1,0:T(1,128)S(1)}, f32[3,1,512]{2,1,0:T(1,128)S(1)}, u32[]{:S(2)}, u32[]{:S(2)}) collective-permute-start(f32[3,1,512]{2,1,0:T(1,128)S(1)} %get-tuple-element.186), channel_id=1, source_target_pairs={{4,0},{8,4},{12,8},{16,12},{20,16},{24,20},{28,24},{5,1},{9,5},{13... | collective-permute-start | bytes 18440 | tf_op jit(solution)/shard_map/ppermute | solution.py:21
  119.9 1.2 copy-start.8
  119.9 1.5 copy-start.9
  119.9 1.8 %copy-start.10 = (f32[512,512]{1,0:T(8,128)S(1)}, f32[512,512]{1,0:T(8,128)}, u32[]{:S(2)}) copy-start(f32[512,512]{1,0:T(8,128)} %param.16) | copy-start | bytes 3145732
  121.8 12.9 %copy-start.7 = (f32[512,512]{1,0:T(8,128)S(1)}, f32[512,512]{1,0:T(8,128)}, u32[]{:S(2)}) copy-start(f32[512,512]{1,0:T(8,128)} %get-tuple-element.129) | copy-start | bytes 3145732
  128.2 7.2 %collective-permute-start.4 = (f32[1,512]{1,0:T(1,128)S(1)}, f32[1,512]{1,0:T(1,128)S(1)}, u32[]{:S(2)}, u32[]{:S(2)}) collective-permute-start(f32[1,512]{1,0:T(1,128)S(1)} %get-tuple-element.189), channel_id=1, source_target_pairs={{0,4},{4,8},{8,12},{12,16},{16,20},{20,24},{24,28},{1,5},{5,9},{9,... | collective-permute-start | bytes 6152 | tf_op jit(solution)/shard_map/ppermute | solution.py:18
  130.4 5.6 %collective-permute-start.5 = (f32[1,512]{1,0:T(1,128)S(1)}, f32[1,512]{1,0:T(1,128)S(1)}, u32[]{:S(2)}, u32[]{:S(2)}) collective-permute-start(f32[1,512]{1,0:T(1,128)S(1)} %get-tuple-element.190), channel_id=1, source_target_pairs={{4,0},{8,4},{12,8},{16,12},{20,16},{24,20},{28,24},{5,1},{9,5},{13... | collective-permute-start | bytes 6152 | tf_op jit(solution)/shard_map/ppermute | solution.py:21
  136.4 8.4 %copy-start.1 = (f32[4,512,512]{2,1,0:T(8,128)S(1)}, f32[4,512,512]{2,1,0:T(8,128)}, u32[]{:S(2)}) copy-start(f32[4,512,512]{2,1,0:T(8,128)} %get-tuple-element.176) | copy-start | bytes 12582916
  138.2 6.7 %collective-permute-start.6 = (f32[1,512]{1,0:T(1,128)S(1)}, f32[1,512]{1,0:T(1,128)S(1)}, u32[]{:S(2)}, u32[]{:S(2)}) collective-permute-start(f32[1,512]{1,0:T(1,128)S(1)} %get-tuple-element.187), channel_id=1, source_target_pairs={{0,4},{4,8},{8,12},{12,16},{16,20},{20,24},{24,28},{1,5},{5,9},{9,... | collective-permute-start | bytes 6152 | tf_op jit(solution)/shard_map/ppermute | solution.py:18
  140.1 5.8 %collective-permute-start.7 = (f32[1,512]{1,0:T(1,128)S(1)}, f32[1,512]{1,0:T(1,128)S(1)}, u32[]{:S(2)}, u32[]{:S(2)}) collective-permute-start(f32[1,512]{1,0:T(1,128)S(1)} %get-tuple-element.188), channel_id=1, source_target_pairs={{4,0},{8,4},{12,8},{16,12},{20,16},{24,20},{28,24},{5,1},{9,5},{13... | collective-permute-start | bytes 6152 | tf_op jit(solution)/shard_map/ppermute | solution.py:21
  150.3 12.0 %copy-start = (f32[4,512,512]{2,1,0:T(8,128)}, f32[4,512,512]{2,1,0:T(8,128)S(1)}, u32[]{:S(2)}) copy-start(f32[4,512,512]{2,1,0:T(8,128)S(1)} %multiply_add_fusion) | copy-start | bytes 12582916
  150.3 11.9 %collective-permute-start.8 = (f32[2,4,512]{2,0,1:T(2,128)S(1)}, f32[2,4,512]{2,0,1:T(2,128)S(1)}, u32[]{:S(2)}, u32[]{:S(2)}) collective-permute-start(f32[2,4,512]{2,0,1:T(2,128)S(1)} %pad_maximum_fusion.13), channel_id=1, source_target_pairs={{4,0},{8,4},{12,8},{16,12},{20,16},{24,20},{28,24},{5,1},{9,5},{13... | collective-permute-start | bytes 49160 | tf_op jit(solution)/shard_map/ppermute | solution.py:29
Sparse Core Ops, SparseCore 0:
  23.9 86.4 all-reduce.10
where the time goes:
time: 177 us
  waiting for transfers between devices  61.2 us (35%)
  other arithmetic  42.7 us (24%)
  starting transfers between devices  30.6 us (17%)
  between operations  15 us (8%)
  local copies, waits for them, and re-layouts  14.7 us (8%)
  blocking collectives  12.4 us (7%)
    psum x1, waiting for transfers between devices, local(): summed = lax.psum(column_parts, 'layer')  59.5 us
    ppermute x4, starting transfers between devices, padded_2(): lax.ppermute(lax.slice_in_dim(block, 0, width, axis=dim), axis, backward)  18.1 us
    unnamed x1, blocking collectives  12.4 us
    div x3, other arithmetic, relax(): return (right_hand + inflow) / diagonal  9.84 us
    ppermute x4, starting transfers between devices, padded_2(): lax.ppermute(lax.slice_in_dim(block, block.shape[dim] - width, None, axis...  7.92 us
    reduce_sum x1, other arithmetic, local(): jnp.sum(conduct, axis=0)  7.77 us
    mul x1, other arithmetic, local(): harmonic(conduct, side_conduct) * (cell_pressure - side_pressure)  7.44 us
    reduce_sum x4, other arithmetic, add_block(): jnp.sum(jnp.where(gas & (depth < limit), thick_block, 0.0), axis=0)  5.35 us
  transfers between devices with their start and end apart: 10, of which 3 were waited for; matrix products, arithmetic and copies ran while one was open for 17% of the time, Pallas kernels for 0%

commit v1 on v0

--- a/solution.py
+++ b/solution.py
@@ -8,6 +8,15 @@
 gravity_scale = 0.05
 gas_density = 0.7
 brine_density = 1.0
+
+
+def doubling_sum(value, mesh_axis):
+    size = lax.axis_size(mesh_axis)
+    total, stride = (value, 1)
+    while stride < size:
+        total = total + lax.ppermute(total, mesh_axis, [(i, i ^ stride) for i in range(size)])
+        stride = 2 * stride
+    return total
 
 
 def padded_2(block, sides, width):
@@ -112,7 +121,7 @@
     column_parts = jnp.stack(
         [jnp.sum(conduct, axis=0), jnp.sum(jnp.where(gas_cell, conduct, 0.0), axis=0)]
     )
-    summed = lax.psum(column_parts, "layer")
+    summed = doubling_sum(column_parts, "layer")
     summed = jnp.concatenate([summed, gas_height[None]], axis=0)
     padded = padded_2(summed, (("area", 1),), 1)
     trans_faces, right_hand, diagonal = prepare(padded, storage, source, pressure_old)

time: 177 us -> 221 us (1.25)
  blocking collectives: 12.4 us -> 42.7 us
  waiting for transfers between devices: 61.2 us -> 80.5 us
  between operations: 15 us -> 1.66 us
  other arithmetic: 42.7 us -> 48 us
    ppermute x0 -> x2, waiting for transfers between devices: none -> 78 us  [doubling_sum(): lax.ppermute(total, mesh_axis, [(i, i ^ stride) for i in range(size)])]
    psum x1 -> x0, waiting for transfers between devices: 59.5 us -> none  [local(): summed = lax.psum(column_parts, 'layer')]
    unnamed x1, blocking collectives: 12.4 us -> 42.7 us
    add x0 -> x2, other arithmetic: none -> 7.52 us  [doubling_sum(): total + lax.ppermute(total, mesh_axis, [(i, i ^ stride) for i in range(si...]
  transfers between devices with their start and end apart: 10 -> 11, of which waited for: 3 -> 4; matrix products, arithmetic and copies ran while one was open for 17% -> 12% of each run, Pallas kernels for 0% -> 0%
where the time goes in v1:
time: 221 us
  waiting for transfers between devices  80.5 us (36%)
  other arithmetic  48 us (22%)
  blocking collectives  42.7 us (19%)
  starting transfers between devices  32.2 us (15%)
  local copies, waits for them, and re-layouts  15.4 us (7%)
    ppermute x2, waiting for transfers between devices, doubling_sum(): lax.ppermute(total, mesh_axis, [(i, i ^ stride) for i in range(size)])  78 us
    unnamed x1, blocking collectives  42.7 us
    ppermute x4, starting transfers between devices, padded_2(): lax.ppermute(lax.slice_in_dim(block, 0, width, axis=dim), axis, backward)  17.7 us
    div x3, other arithmetic, relax(): return (right_hand + inflow) / diagonal  9.84 us
    ppermute x4, starting transfers between devices, padded_2(): lax.ppermute(lax.slice_in_dim(block, block.shape[dim] - width, None, axis...  8.46 us
    reduce_sum x1, other arithmetic, local(): jnp.sum(conduct, axis=0)  7.77 us
    add x2, other arithmetic, doubling_sum(): total + lax.ppermute(total, mesh_axis, [(i, i ^ stride) for i in range(si...  7.52 us
    mul x1, other arithmetic, local(): harmonic(conduct, side_conduct) * (cell_pressure - side_pressure)  7.44 us
  transfers between devices with their start and end apart: 11, of which 4 were waited for; matrix products, arithmetic and copies ran while one was open for 12% of the time, Pallas kernels for 0%

profile of v1, /device:TPU:4, one launch (start us, length us, event | category | flops | bytes accessed | tf_op | source)
XLA Modules:
  0.0 220.7 jit_solution(15150886650092543474)
XLA Ops:
  0.6 7.8 %fusion.60 = (f32[512,512]{1,0:T(8,128)S(1)}, f32[512,512]{1,0:T(8,128)S(1)}, f32[4,512,512]{2,1,0:T(8,128)}) fusion(s32[512,512]{1,0:T(8,128)} %param.14, s32[512,512]{1,0:T(8,128)} %param.13, s32[4]{0:T(128)S(1)} %iota_add_fusion.1, f32[4]{0:T(128)} %param.12, f32[4,512,512]{2,1,0:T(8,128)} %param.10, f32[4,512,512]{2,1,0:T(8,128)} %param.11), kind=kLoop, calls=%fused_computation.139 | loop fusion | flops 8912896 | bytes 16777248 | tf_op jit(solution)/shard_map/reduce_sum | solution.py:122
  8.4 1.0 copy-done.7
  9.4 1.5 pad_maximum_fusion.2
  10.9 1.6 collective-permute-start
  12.5 0.7 fusion.66
  13.2 1.9 collective-permute-start.4
  15.2 4.5 %collective-permute-start.5 = (f32[1,512]{1,0:T(1,128)S(1)}, f32[1,512]{1,0:T(1,128)S(1)}, u32[]{:S(2)}, u32[]{:S(2)}) collective-permute-start(f32[1,512]{1,0:T(1,128)S(1)} %get-tuple-element.192), channel_id=1, source_target_pairs={{4,0},{8,4},{12,8},{16,12},{20,16},{24,20},{28,24},{5,1},{9,5},{13... | collective-permute-start | bytes 6152 | tf_op jit(solution)/shard_map/ppermute | solution.py:30
  19.7 0.6 dynamic-slice
  21.2 42.7 %all-reduce.8 = f32[16]{0:T(128)S(1)} all-reduce(f32[16]{0:T(128)S(1)} %dynamic-update-slice), channel_id=1, replica_groups=mesh['area'=8,'layer'=4] {'layer'}, use_global_device_ids=true, to_apply=%add.8 | all-reduce | flops 16 | bytes 128
  63.9 4.0 %fusion.59 = f32[2,512,512]{2,1,0:T(8,128)} fusion(f32[2,512,512]{2,1,0:T(8,128)} %collective-permute-done, f32[1,512,512]{2,1,0:T(8,128)} %bitcast.93, f32[1,512,512]{2,1,0:T(8,128)} %bitcast.90), kind=kLoop, calls=%fused_computation.138 | loop fusion | flops 1048576 | bytes 6291456 | tf_op jit(solution)/shard_map/add | solution.py:17
  67.9 12.6 %while.16 = (s32[]{:T(128)}, f32[512,512]{1,0:T(8,128)S(1)}, f32[512,512]{1,0:T(8,128)}, s32[512,512]{1,0:T(8,128)S(1)}, s32[512,512]{1,0:T(8,128)S(1)}, /*index...) while((s32[]{:T(128)}, f32[512,512]{1,0:T(8,128)S(1)}, ...), condition=%wide.region_5.6_spmd.clone, body=%wide.region_2.5_spmd.clone.sunk | while | flops 8912915 | bytes 18874700 | solution.py:107
  68.0 1.3 select_reduce_fusion.4
  69.4 0.7 select_add_fusion.3
  70.1 1.0 copy-done.5
  71.2 1.3 select_reduce_fusion.4
  72.5 0.7 select_add_fusion.3
  73.3 1.0 copy-done.5
  74.3 1.3 select_reduce_fusion.4
  75.7 0.7 select_add_fusion.3
  76.4 1.0 copy-done.5
  77.5 1.3 select_reduce_fusion.4
  78.8 0.7 select_add_fusion.3
  79.6 1.0 copy-done.5
  80.5 0.6 fusion.55
  81.2 78.0 %collective-permute-done.1 = f32[2,512,512]{2,1,0:T(8,128)} collective-permute-done((f32[2,512,512]{2,1,0:T(8,128)}, f32[2,512,512]{2,1,0:T(8,128)}, u32[]{:S(2)}, u32[]{:S(2)}) %collective-permute-start.1) | collective-permute-done | bytes 2097184 | tf_op jit(solution)/shard_map/ppermute | solution.py:17
  159.2 3.6 %fusion.67 = f32[2,512,512]{2,1,0:T(8,128)S(1)} fusion(f32[2,512,512]{2,1,0:T(8,128)} %collective-permute-done.1, f32[2,512,512]{2,1,0:T(8,128)} %collective-permute-done, f32[1,512,512]{2,1,0:T(8,128)} %bitcast.94, f32[1,512,512]{2,1,0:T(8,128)} %bitcast.91), kind=kLoop, calls=%fused_computation.143 | loop fusion | flops 1572864 | bytes 8388608 | tf_op jit(solution)/shard_map/add | solution.py:17
  162.7 2.1 collective-permute-start.2
  164.8 4.5 %collective-permute-start.3 = (f32[3,1,512]{2,1,0:T(1,128)S(1)}, f32[3,1,512]{2,1,0:T(1,128)S(1)}, u32[]{:S(2)}, u32[]{:S(2)}) collective-permute-start(f32[3,1,512]{2,1,0:T(1,128)S(1)} %get-tuple-element.186), channel_id=1, source_target_pairs={{4,0},{8,4},{12,8},{16,12},{20,16},{24,20},{28,24},{5,1},{9,5},{13... | collective-permute-start | bytes 18440 | tf_op jit(solution)/shard_map/ppermute | solution.py:30
  169.4 0.4 select_maximum_fusion.4
  169.8 0.8 collective-permute-done.3
  171.5 0.8 copy-done.9
  172.6 6.4 %fusion.46 = (f32[512,512]{1,0:T(8,128)S(1)}, f32[512,512]{1,0:T(8,128)S(1)}, f32[512,512]{1,0:T(8,128)S(1)}, f32[512,512]{1,0:T(8,128)S(1)}) fusion(f32[514,514]{1,0:T(8,128)S(1)} %select_maximum_fusion.4, f32[1,512]{1,0:T(1,128)S(1)} %collective-permute-done.5, f32[512,512]{1,0:T(8,128)S(1)} %copy-done.10, f32[1,512]{1,0:T(1,128)S(1)} %collective-permute-done.4, ...), kind=kLoop, calls=%fused_computation.98 | loop fusion | flops 20709376 | bytes 21037056 | tf_op jit(solution)/shard_map/div | solution.py:90
  179.1 2.6 %collective-permute-start.6 = (f32[1,512]{1,0:T(1,128)S(1)}, f32[1,512]{1,0:T(1,128)S(1)}, u32[]{:S(2)}, u32[]{:S(2)}) collective-permute-start(f32[1,512]{1,0:T(1,128)S(1)} %get-tuple-element.189), channel_id=1, source_target_pairs={{0,4},{4,8},{8,12},{12,16},{16,20},{20,24},{24,28},{1,5},{5,9},{9,... | collective-permute-start | bytes 6152 | tf_op jit(solution)/shard_map/ppermute | solution.py:27
  181.7 3.9 %collective-permute-start.7 = (f32[1,512]{1,0:T(1,128)S(1)}, f32[1,512]{1,0:T(1,128)S(1)}, u32[]{:S(2)}, u32[]{:S(2)}) collective-permute-start(f32[1,512]{1,0:T(1,128)S(1)} %get-tuple-element.190), channel_id=1, source_target_pairs={{4,0},{8,4},{12,8},{16,12},{20,16},{24,20},{28,24},{5,1},{9,5},{13... | collective-permute-start | bytes 6152 | tf_op jit(solution)/shard_map/ppermute | solution.py:30
  185.6 0.7 multiply_subtract_fusion
  186.3 0.6 collective-permute-done.7
  187.3 1.7 fusion.39
  189.0 1.9 collective-permute-start.8
  191.0 4.7 %collective-permute-start.9 = (f32[1,512]{1,0:T(1,128)S(1)}, f32[1,512]{1,0:T(1,128)S(1)}, u32[]{:S(2)}, u32[]{:S(2)}) collective-permute-start(f32[1,512]{1,0:T(1,128)S(1)} %get-tuple-element.188), channel_id=1, source_target_pairs={{4,0},{8,4},{12,8},{16,12},{20,16},{24,20},{28,24},{5,1},{9,5},{13... | collective-permute-start | bytes 6152 | tf_op jit(solution)/shard_map/ppermute | solution.py:30
  195.7 1.1 collective-permute-done.9
  197.3 1.7 fusion.32
  199.0 2.2 multiply_add_fusion
  201.2 4.5 %collective-permute-start.10 = (f32[2,4,512]{2,0,1:T(2,128)S(1)}, f32[2,4,512]{2,0,1:T(2,128)S(1)}, u32[]{:S(2)}, u32[]{:S(2)}) collective-permute-start(f32[2,4,512]{2,0,1:T(2,128)S(1)} %pad_maximum_fusion.13), channel_id=1, source_target_pairs={{4,0},{8,4},{12,8},{16,12},{20,16},{24,20},{28,24},{5,1},{9,5},{13... | collective-permute-start | bytes 49160 | tf_op jit(solution)/shard_map/ppermute | solution.py:38
  205.7 0.7 slice.276
  206.4 1.1 slice.282
  207.5 3.1 %slice.283 = f32[4,512,511]{2,1,0:T(8,128)} slice(f32[4,512,512]{2,1,0:T(8,128)S(1)} %multiply_add_fusion), slice={[0:4], [0:512], [1:512]} | slice | bytes 8372224 | tf_op jit(solution)/shard_map/slice | solution.py:144
  210.7 2.5 %slice.280 = f32[4,511,512]{2,1,0:T(8,128)} slice(f32[4,512,512]{2,1,0:T(8,128)S(1)} %multiply_add_fusion), slice={[0:4], [1:512], [0:512]} | slice | bytes 8372224 | tf_op jit(solution)/shard_map/slice | solution.py:141
  213.2 7.4 %fusion.3 = (f32[4,512,512]{2,1,0:T(8,128)}, f32[4,512,512]{2,1,0:T(8,128)}) fusion(f32[4,512,512]{2,1,0:T(8,128)S(1)} %multiply_add_fusion, f32[4,512,511]{2,1,0:T(8,128)} %slice.283, f32[4,512,512]{2,1,0:T(8,128)S(1)} %copy-done.1, f32[4,512,511]{2,1,0:T(8,128)S(1)} %slice.282, f32[4,1,512]{2,1,0:T(1,128)S(1)} %get-tuple-element.194, ...), kind=kLoop, calls=%fused_computation.14 | loop fusion | flops 17825792 | bytes 33538048 | tf_op jit(solution)/shard_map/mul | solution.py:145
  (70 shorter events, 2.8 us)
Async XLA Ops:
  8.4 1.0 copy-start.7
  8.4 2.5 %copy-start.8 = (f32[512,512]{1,0:T(8,128)}, f32[512,512]{1,0:T(8,128)S(1)}, u32[]{:S(2)}) copy-start(f32[512,512]{1,0:T(8,128)S(1)} %get-tuple-element.157) | copy-start | bytes 3145732
  8.4 11.3 %copy-start.13 = (u32[32]{0:T(128)S(1)}, u32[32]{0:T(128)}, u32[]{:S(2)}) copy-start(u32[32]{0:T(128)} %constant.82) | copy-start | bytes 388
  8.4 12.6 %copy-start.12 = (f32[4]{0:T(128)S(1)}, f32[4]{0:T(128)}, u32[]{:S(2)}) copy-start(f32[4]{0:T(128)} %param.12) | copy-start | bytes 52
  10.9 57.0 %copy-start.2 = (s32[512,512]{1,0:T(8,128)S(1)}, s32[512,512]{1,0:T(8,128)}, u32[]{:S(2)}) copy-start(s32[512,512]{1,0:T(8,128)} %param.13) | copy-start | bytes 3145732
  10.9 57.0 %copy-start.3 = (s32[512,512]{1,0:T(8,128)S(1)}, s32[512,512]{1,0:T(8,128)}, u32[]{:S(2)}) copy-start(s32[512,512]{1,0:T(8,128)} %param.14) | copy-start | bytes 3145732
  10.9 53.0 %collective-permute-start = (f32[2,512,512]{2,1,0:T(8,128)}, f32[2,512,512]{2,1,0:T(8,128)}, u32[]{:S(2)}, u32[]{:S(2)}) collective-permute-start(f32[2,512,512]{2,1,0:T(8,128)} %pad_maximum_fusion.2), channel_id=1, source_target_pairs={{0,1},{1,0},{2,3},{3,2},{4,5},{5,4},{6,7},{7,6},{8,9},{9,8},{10,11... | collective-permute-start | bytes 6291464 | tf_op jit(solution)/shard_map/ppermute | solution.py:17
  13.2 156.1 %collective-permute-start.4 = (f32[1,512]{1,0:T(1,128)S(1)}, f32[1,512]{1,0:T(1,128)S(1)}, u32[]{:S(2)}, u32[]{:S(2)}) collective-permute-start(f32[1,512]{1,0:T(1,128)S(1)} %get-tuple-element.191), channel_id=1, source_target_pairs={{0,4},{4,8},{8,12},{12,16},{16,20},{20,24},{24,28},{1,5},{5,9},{9,... | collective-permute-start | bytes 6152 | tf_op jit(solution)/shard_map/ppermute | solution.py:27
  15.2 154.2 %collective-permute-start.5 = (f32[1,512]{1,0:T(1,128)S(1)}, f32[1,512]{1,0:T(1,128)S(1)}, u32[]{:S(2)}, u32[]{:S(2)}) collective-permute-start(f32[1,512]{1,0:T(1,128)S(1)} %get-tuple-element.192), channel_id=1, source_target_pairs={{4,0},{8,4},{12,8},{16,12},{20,16},{24,20},{28,24},{5,1},{9,5},{13... | collective-permute-start | bytes 6152 | tf_op jit(solution)/shard_map/ppermute | solution.py:30
  67.9 91.2 %collective-permute-start.1 = (f32[2,512,512]{2,1,0:T(8,128)}, f32[2,512,512]{2,1,0:T(8,128)}, u32[]{:S(2)}, u32[]{:S(2)}) collective-permute-start(f32[2,512,512]{2,1,0:T(8,128)} %fusion.59), channel_id=1, source_target_pairs={{0,2},{1,3},{2,0},{3,1},{4,6},{5,7},{6,4},{7,5},{8,10},{9,11},{10,... | collective-permute-start | bytes 6291464 | tf_op jit(solution)/shard_map/ppermute | solution.py:17
  67.9 1.4 copy-start.4
  70.1 1.0 copy-start.5
  71.1 1.4 copy-start.4
  73.3 1.0 copy-start.5
  74.3 1.4 copy-start.4
  76.4 1.0 copy-start.5
  77.4 1.4 copy-start.4
  79.6 1.0 copy-start.5
  162.7 6.7 %copy-start.10 = (f32[512,512]{1,0:T(8,128)S(1)}, f32[512,512]{1,0:T(8,128)}, u32[]{:S(2)}) copy-start(f32[512,512]{1,0:T(8,128)} %param.17) | copy-start | bytes 3145732
  162.7 7.1 %collective-permute-start.2 = (f32[3,1,512]{2,1,0:T(1,128)S(1)}, f32[3,1,512]{2,1,0:T(1,128)S(1)}, u32[]{:S(2)}, u32[]{:S(2)}) collective-permute-start(f32[3,1,512]{2,1,0:T(1,128)S(1)} %get-tuple-element.185), channel_id=1, source_target_pairs={{0,4},{4,8},{8,12},{12,16},{16,20},{20,24},{24,28},{1,5},{5,9},{9,... | collective-permute-start | bytes 18440 | tf_op jit(solution)/shard_map/ppermute | solution.py:27
  164.8 5.9 %collective-permute-start.3 = (f32[3,1,512]{2,1,0:T(1,128)S(1)}, f32[3,1,512]{2,1,0:T(1,128)S(1)}, u32[]{:S(2)}, u32[]{:S(2)}) collective-permute-start(f32[3,1,512]{2,1,0:T(1,128)S(1)} %get-tuple-element.186), channel_id=1, source_target_pairs={{4,0},{8,4},{12,8},{16,12},{20,16},{24,20},{28,24},{5,1},{9,5},{13... | collective-permute-start | bytes 18440 | tf_op jit(solution)/shard_map/ppermute | solution.py:30
  171.1 1.2 copy-start.9
  171.1 1.5 copy-start.11
  172.6 12.9 %copy-start.6 = (f32[512,512]{1,0:T(8,128)S(1)}, f32[512,512]{1,0:T(8,128)}, u32[]{:S(2)}) copy-start(f32[512,512]{1,0:T(8,128)} %get-tuple-element.129) | copy-start | bytes 3145732
  179.1 7.2 %collective-permute-start.6 = (f32[1,512]{1,0:T(1,128)S(1)}, f32[1,512]{1,0:T(1,128)S(1)}, u32[]{:S(2)}, u32[]{:S(2)}) collective-permute-start(f32[1,512]{1,0:T(1,128)S(1)} %get-tuple-element.189), channel_id=1, source_target_pairs={{0,4},{4,8},{8,12},{12,16},{16,20},{20,24},{24,28},{1,5},{5,9},{9,... | collective-permute-start | bytes 6152 | tf_op jit(solution)/shard_map/ppermute | solution.py:27
  181.7 5.2 %collective-permute-start.7 = (f32[1,512]{1,0:T(1,128)S(1)}, f32[1,512]{1,0:T(1,128)S(1)}, u32[]{:S(2)}, u32[]{:S(2)}) collective-permute-start(f32[1,512]{1,0:T(1,128)S(1)} %get-tuple-element.190), channel_id=1, source_target_pairs={{4,0},{8,4},{12,8},{16,12},{20,16},{24,20},{28,24},{5,1},{9,5},{13... | collective-permute-start | bytes 6152 | tf_op jit(solution)/shard_map/ppermute | solution.py:30
  187.3 8.4 %copy-start.1 = (f32[4,512,512]{2,1,0:T(8,128)S(1)}, f32[4,512,512]{2,1,0:T(8,128)}, u32[]{:S(2)}) copy-start(f32[4,512,512]{2,1,0:T(8,128)} %get-tuple-element.176) | copy-start | bytes 12582916
  189.0 6.7 %collective-permute-start.8 = (f32[1,512]{1,0:T(1,128)S(1)}, f32[1,512]{1,0:T(1,128)S(1)}, u32[]{:S(2)}, u32[]{:S(2)}) collective-permute-start(f32[1,512]{1,0:T(1,128)S(1)} %get-tuple-element.187), channel_id=1, source_target_pairs={{0,4},{4,8},{8,12},{12,16},{16,20},{20,24},{24,28},{1,5},{5,9},{9,... | collective-permute-start | bytes 6152 | tf_op jit(solution)/shard_map/ppermute | solution.py:27
  191.0 5.8 %collective-permute-start.9 = (f32[1,512]{1,0:T(1,128)S(1)}, f32[1,512]{1,0:T(1,128)S(1)}, u32[]{:S(2)}, u32[]{:S(2)}) collective-permute-start(f32[1,512]{1,0:T(1,128)S(1)} %get-tuple-element.188), channel_id=1, source_target_pairs={{4,0},{8,4},{12,8},{16,12},{20,16},{24,20},{28,24},{5,1},{9,5},{13... | collective-permute-start | bytes 6152 | tf_op jit(solution)/shard_map/ppermute | solution.py:30
  201.2 12.0 %copy-start = (f32[4,512,512]{2,1,0:T(8,128)}, f32[4,512,512]{2,1,0:T(8,128)S(1)}, u32[]{:S(2)}) copy-start(f32[4,512,512]{2,1,0:T(8,128)S(1)} %multiply_add_fusion) | copy-start | bytes 12582916
  201.2 12.0 %collective-permute-start.10 = (f32[2,4,512]{2,0,1:T(2,128)S(1)}, f32[2,4,512]{2,0,1:T(2,128)S(1)}, u32[]{:S(2)}, u32[]{:S(2)}) collective-permute-start(f32[2,4,512]{2,0,1:T(2,128)S(1)} %pad_maximum_fusion.13), channel_id=1, source_target_pairs={{4,0},{8,4},{12,8},{16,12},{20,16},{24,20},{28,24},{5,1},{9,5},{13... | collective-permute-start | bytes 49160 | tf_op jit(solution)/shard_map/ppermute | solution.py:38
